TPU v7x, 512 devices: a whole 4x4x16 slice. The times are simulated.
512 devices in a mesh: grp: 16 (over z), blk: 32 (over x, y, core).
Axes of the slice: x: 4, y: 4, z: 16, core: 2. Of those that a mesh axis runs over, the one named last changes fastest.
Arguments:
- ancestor_inv: float32 [16, 6144, 3072], P('grp', 'blk'), as said below
- lower_block: float32 [16, 3840, 768], P('grp', 'blk'), may hold values from -0.009765625 to 0.009765625
- diag_inverse: float32 [16, 768, 768], P('grp', 'blk'), as said below
- row_index: int32 [16, 3840], P('grp'), may hold values from 0 to 6143, as said below
Outputs:
- sigma_rows: float32 [16, 3840, 768], P('grp', 'blk')
- sigma_diag: float32 [16, 768, 768], P('grp', 'blk')
Inputs may be any that keep to these rules, and one draw needn't show every extreme that they name: `row_index`: for each child front: sorted increasing and distinct; exactly 120 entries fall in each aligned block of 192 consecutive indices, among them the block's first and last index. `diag_inverse`: lower triangular with a positive diagonal. `ancestor_inv`: each parent matrix assembled from its two column halves is symmetric.
All inputs are finite; a program needn't handle non-finite values.
Results may differ from a plain program's by a relative error of at most 0.0003.
Values sent between devices are 32-bit elements; how exact they have to be, the bound alone decides.
A program may use at most 64 MiB of HBM per device.

v0:
```python
import jax
import jax.numpy as jnp
from jax import lax
from jax.sharding import PartitionSpec as P


def partner(x, axis, stride):
    return lax.ppermute(x, axis, [(i, i ^ 1 << stride) for i in range(lax.axis_size(axis))])


def shards(ancestor_inv, lower_block, diag_inverse, row_index):
    highest = lax.Precision.HIGHEST
    blk_count = lax.axis_size("blk")
    tile_rows = ancestor_inv.shape[1]
    half_cols = ancestor_inv.shape[2]
    tile = ancestor_inv[0]
    listed = row_index[0]
    total_rows = listed.shape[0]
    picked = total_rows // blk_count
    half_rows = total_rows // 2
    blk_here = lax.axis_index("blk")
    side = lax.axis_index("grp") % 2
    other_side = 1 - side

    def pick_panel(source, names, col_side):
        rows_here = (
            lax.dynamic_slice_in_dim(names, blk_here * picked, picked) - blk_here * tile_rows
        )
        cols_here = (
            lax.dynamic_slice_in_dim(names, col_side * half_rows, half_rows) - col_side * half_cols
        )
        return jnp.take(jnp.take(source, rows_here, axis=0), cols_here, axis=1)

    own_part = pick_panel(tile, listed, side)
    partner_tile = partner(tile, "grp", 0)
    other_part = pick_panel(partner_tile, listed, other_side)
    low_first = jnp.concatenate([own_part, other_part], axis=1)
    high_first = jnp.concatenate([other_part, own_part], axis=1)
    row_panel = jnp.where(side == 0, low_first, high_first)
    pivot_full = lax.all_gather(diag_inverse, "blk", axis=1, tiled=True)
    factor = jnp.einsum("kra,kab->krb", lower_block, pivot_full, precision=highest)
    product = jnp.einsum(
        "rn,knb->krb",
        row_panel,
        lax.all_gather(factor, "blk", axis=1, tiled=True),
        precision=highest,
    )
    sigma_rows = -product
    cross_terms = jnp.einsum("krb,krc->kbc", factor, sigma_rows, precision=highest)
    reduced = lax.psum_scatter(cross_terms, "blk", scatter_dimension=1, tiled=True)
    row_width = reduced.shape[1]
    gram_cols = lax.dynamic_slice_in_dim(pivot_full, blk_here * row_width, row_width, 2)
    gram_rows = jnp.einsum("kar,kac->krc", gram_cols, pivot_full, precision=highest)
    sigma_diag = gram_rows - reduced
    return (sigma_rows, sigma_diag)


def solution(mesh):
    in_specs = (P("grp", "blk", None), P("grp", "blk", None), P("grp", "blk", None), P("grp", None))
    out_specs = (P("grp", "blk", None), P("grp", "blk", None))
    return jax.shard_map(shards, mesh=mesh, in_specs=in_specs, out_specs=out_specs, check_vma=False)
```

profile of v0, /device:TPU:2, one launch (start us, length us, event | category | flops | bytes accessed | tf_op | source)
XLA Modules:
  0.0 283.2 jit_solution(15256217168831893041)
XLA Ops:
  7.2 0.0 copy-start
  7.2 0.0 copy-start.1
  7.2 0.0 copy-start.7
  7.2 0.0 all-gather.4.cloned.1.call-start
  7.2 0.7 all-gather.4.cloned.1.call-update
  7.9 0.0 all-gather.6.cloned.1.call-start
  8.0 66.9 %all-gather.4.cloned.1.call-done = f32[1,768,768]{2,1,0:T(8,128)} async-done(((f32[1,24,768]{2,1,0:T(8,128)}), f32[1,768,768]{2,1,0:T(8,128)}) %all-gather.4.cloned.1.call-update) | async-done | bytes 2359312 | tf_op jit(solution)/shard_map/all_gather | solution.py:40
  74.9 0.0 copy-done
  74.9 3.8 %fusion.2 = f32[120,768]{1,0:T(8,128)} fusion(f32[1,768,768]{2,1,0:T(8,128)} %all-gather.4.cloned.1.call-done, f32[1,120,768]{2,1,0:T(8,128)S(1)} %copy-done), kind=kOutput, calls=%fused_computation.6 | convolution fusion | flops 849346560 | bytes 3096576 | tf_op jit(solution)/shard_map/kra,kab->krb/dot_general | solution.py:41
  78.7 0.0 all-gather.6.cloned.1.call-update
  78.7 0.0 reduce-scatter.2.cloned.1.call-start
  78.7 0.0 copy-done.1
  78.7 3.5 %collective-permute-start = (f32[192,3072]{1,0:T(8,128)S(1)}, f32[192,3072]{1,0:T(8,128)}, u32[]{:S(2)}, u32[]{:S(2)}) collective-permute-start(f32[192,3072]{1,0:T(8,128)S(1)} %bitcast.40), channel_id=1, source_target_pairs={{0,32},{32,0},{64,96},{96,64},{128,160},{160,128},{192,224},{224,1... | collective-permute-start | bytes 7077896 | tf_op jit(solution)/shard_map/ppermute | solution.py:8
  82.3 0.1 compare_and_fusion.2
  82.3 2.2 gather_fusion
  84.7 49.5 %collective-permute-done = f32[192,3072]{1,0:T(8,128)} collective-permute-done((f32[192,3072]{1,0:T(8,128)S(1)}, f32[192,3072]{1,0:T(8,128)}, u32[]{:S(2)}, u32[]{:S(2)}) %collective-permute-start) | collective-permute-done | bytes 2359328 | tf_op jit(solution)/shard_map/ppermute | solution.py:8
  134.2 3.6 %gather_fusion.2 = f32[120,3072]{1,0:T(8,128)S(1)} fusion(f32[192,3072]{1,0:T(8,128)} %collective-permute-done, s32[1024]{0:T(1024)S(1)} %pad_clamp_fusion.2), kind=kCustom, calls=%fused_computation.2.clone | custom fusion | bytes 2949600 | tf_op jit(solution)/shard_map/jit(_take)/gather | solution.py:32
  137.8 2.0 broadcast_select_fusion.1
  139.8 2.0 copy.6
  141.8 2.0 copy.7
  143.8 4.5 %gather_fusion.1 = f32[1920,120]{1,0:T(8,128)} fusion(f32[120,3072]{0,1:T(8,128)S(1)} %copy.6, s32[2048]{0:T(1024)S(1)} %pad_clamp_fusion.1), kind=kCustom, calls=%fused_computation.1.clone | custom fusion | bytes 1850880 | tf_op jit(solution)/shard_map/jit(_take)/gather | solution.py:32
  148.4 4.5 %gather_fusion.3 = f32[1920,120]{1,0:T(8,128)} fusion(f32[120,3072]{0,1:T(8,128)S(1)} %copy.7, s32[2048]{0:T(1024)S(1)} %pad_clamp_fusion), kind=kCustom, calls=%fused_computation.3.clone | custom fusion | bytes 1850880 | tf_op jit(solution)/shard_map/jit(_take)/gather | solution.py:32
  152.9 1.6 select_bitcast_fusion.1
  154.5 0.3 select_bitcast_fusion
  154.8 0.0 copy-start.5
  154.8 0.1 all-gather.6.cloned.1.call-done
  155.0 13.4 %fusion.10 = f32[768,120]{0,1:T(8,128)S(1)} fusion(f32[3840,768]{1,0:T(8,128)} %all-gather.6.cloned.1.call-done, f32[120,1920]{0,1:T(8,128)S(1)} %select_bitcast_fusion, f32[120,1920]{0,1:T(8,128)S(1)} %select_bitcast_fusion.1, pred[]{:T(512)S(6)} %eq.5), kind=kOutput, calls=%fused_computation.16 | convolution fusion | flops 4248207360 | bytes 14008321 | tf_op jit(solution)/shard_map/rn,knb->krb/dot_general | solution.py:42
  168.4 0.0 copy-start.6
  168.4 3.5 %convolution_bitcast_fusion = f32[1,768,768]{2,1,0:T(8,128)} fusion(f32[120,768]{1,0:T(8,128)S(1)} %copy-done.5, f32[768,120]{0,1:T(8,128)S(1)} %fusion.10), kind=kOutput, calls=%fused_computation.15 | convolution fusion | flops 849346560 | bytes 3096576 | tf_op jit(solution)/shard_map/krb,krc->kbc/dot_general | solution.py:49
  171.9 0.0 reduce-scatter.2.cloned.1.call-update
  171.9 101.8 %reduce-scatter.2.cloned.1.call-done = f32[1,24,768]{2,1,0:T(8,128)} async-done(((f32[1,768,768]{2,1,0:T(8,128)}), f32[1,24,768]{2,1,0:T(8,128)}) %reduce-scatter.2.cloned.1.call-update) | async-done | bytes 73744 | tf_op jit(solution)/shard_map/reduce_scatter | solution.py:50
  273.8 2.9 %fusion.14 = f32[1,24,768]{2,1,0:T(8,128)} fusion(f32[1,24,768]{2,1,0:T(8,128)} %reduce-scatter.2.cloned.1.call-done, f32[1,768,768]{2,1,0:T(8,128)S(1)} %copy-done.2, s32[]{:T(128)S(6)} %select_n.48), kind=kOutput, calls=%fused_computation.18 | convolution fusion | flops 169887744 | bytes 2899972 | tf_op jit(solution)/shard_map/kar,kac->krc/dot_general | solution.py:53
  (15 shorter events, 0.1 us)
Async XLA Ops:
  7.2 67.7 %copy-start = (f32[1,120,768]{2,1,0:T(8,128)S(1)}, f32[1,120,768]{2,1,0:T(8,128)}, u32[]{:S(2)}) copy-start(f32[1,120,768]{2,1,0:T(8,128)} %param.9) | copy-start | bytes 1105924
  7.2 71.6 %copy-start.1 = (f32[1,192,3072]{2,1,0:T(8,128)S(1)}, f32[1,192,3072]{2,1,0:T(8,128)}, u32[]{:S(2)}) copy-start(f32[1,192,3072]{2,1,0:T(8,128)} %param.8) | copy-start | bytes 7077892
  7.2 75.1 %copy-start.7 = (s32[1,3840]{1,0:T(1,128)S(1)}, s32[1,3840]{1,0:T(1,128)}, u32[]{:S(2)}) copy-start(s32[1,3840]{1,0:T(1,128)} %param.11) | copy-start | bytes 46084
  7.2 67.7 %all-gather.4.cloned.1.call-start = ((), (), s32[]{:S(2)}) async-start(), calls=%async_computation.1 | async-start | bytes 2433024 | tf_op jit(solution)/shard_map/all_gather | solution.py:40
  7.9 147.0 %all-gather.6.cloned.1.call-start = ((), (), s32[]{:S(2)}) async-start(), calls=%async_computation.3 | async-start | bytes 12165120 | tf_op jit(solution)/shard_map/all_gather | solution.py:45
  78.7 195.1 %reduce-scatter.2.cloned.1.call-start = ((), (), s32[]{:S(2)}) async-start(), calls=%async_computation.2 | async-start | bytes 2433024 | tf_op jit(solution)/shard_map/reduce_scatter | solution.py:50
  78.7 55.4 %collective-permute-start = (f32[192,3072]{1,0:T(8,128)S(1)}, f32[192,3072]{1,0:T(8,128)}, u32[]{:S(2)}, u32[]{:S(2)}) collective-permute-start(f32[192,3072]{1,0:T(8,128)S(1)} %bitcast.40), channel_id=1, source_target_pairs={{0,32},{32,0},{64,96},{96,64},{128,160},{160,128},{192,224},{224,1... | collective-permute-start | bytes 7077896 | tf_op jit(solution)/shard_map/ppermute | solution.py:8
  134.2 3.6 %copy-start.3 = (f32[120,3072]{1,0:T(8,128)S(1)}, f32[120,3072]{1,0:T(8,128)}, u32[]{:S(2)}) copy-start(f32[120,3072]{1,0:T(8,128)} %gather_fusion) | copy-start | bytes 4423684
  152.9 1.6 copy-start.4
  154.8 13.6 %copy-start.5 = (f32[120,768]{1,0:T(8,128)S(1)}, f32[120,768]{1,0:T(8,128)}, u32[]{:S(2)}) copy-start(f32[120,768]{1,0:T(8,128)} %fusion.2) | copy-start | bytes 1105924
  168.4 3.6 %copy-start.6 = (f32[768,120]{0,1:T(8,128)}, f32[768,120]{0,1:T(8,128)S(1)}, u32[]{:S(2)}) copy-start(f32[768,120]{0,1:T(8,128)S(1)} %fusion.10) | copy-start | bytes 1105924
  168.4 105.4 %copy-start.2 = (f32[1,768,768]{2,1,0:T(8,128)S(1)}, f32[1,768,768]{2,1,0:T(8,128)}, u32[]{:S(2)}) copy-start(f32[1,768,768]{2,1,0:T(8,128)} %all-gather.4.cloned.1.call-done) | copy-start | bytes 7077892
Sparse Core Ops, SparseCore 0:
  11.2 63.6 all-gather.3
  78.8 76.1 all-gather.5
  172.1 101.6 reduce-scatter.1
where the time goes:
time: 284 us; the launch traced here: 283 us
  waiting for transfers between devices  219 us (77%)
  matrix products  23.6 us (8%)
  local copies, waits for them, and re-layouts  18.9 us (7%)
  between operations  14 us (5%)
  other arithmetic  4.04 us (1%)
  starting transfers between devices  3.58 us (1%)
    reduce_scatter x1, waiting for transfers between devices, shards(): lax.psum_scatter(cross_terms, 'blk', scatter_dimension=1, tiled=True)  102 us
    all_gather x1, waiting for transfers between devices, shards(): pivot_full = lax.all_gather(diag_inverse, 'blk', axis=1, tiled=True)  66.9 us
    ppermute x1, waiting for transfers between devices, partner(): lax.ppermute(x, axis, [(i, i ^ 1 << stride) for i in range(lax.axis_size(...  49.5 us
    gather x4, local copies, waits for them, and re-layouts, pick_panel(): return jnp.take(jnp.take(source, rows_here, axis=0), cols_here, axis=1)  14.9 us
    dot_general x1, matrix products, shards(): jnp.einsum('rn,knb->krb', row_panel, lax.all_gather(factor, 'blk', axis=1...  13.4 us
  transfers between devices with their start and end apart: 4, of which 4 were waited for; matrix products, arithmetic and copies ran while one was open for 8% of the time, Pallas kernels for 0%

commit v1 on v0

v1 whole, which is shorter than its diff:
```python
import jax
import jax.numpy as jnp
from jax import lax
from jax.experimental import pallas as pl
from jax.experimental.pallas import tpu as pltpu
from jax.sharding import PartitionSpec as P

MESH = pl.DeviceIdType.MESH
F32 = jnp.float32
BF16 = jnp.bfloat16
ROWS_L, ROWS_D = 120, 24
PACK = ROWS_L + ROWS_D
HALF = PACK // 2
PAD = 128


def split(v):
    hi = v.astype(BF16)
    lo = (v - hi.astype(F32)).astype(BF16)
    return hi, lo


def dot(a, b):
    return jnp.dot(a, b, preferred_element_type=F32)


def dot_t(a, b):
    return lax.dot_general(a, b, (((0,), (0,)), ((), ())), preferred_element_type=F32)


def body(tile_hbm, low_hbm, dinv_hbm, idx_hbm, rows_out, diag_out,
         tile, idx, idx_sib, picked, panel_send, panel_recv, s_hi, s_lo, packets, acc,
         d_full, part, r1_recv, r1, t1, t2, r2, t3, rows_buf,
         local_sems, send_sems, recv_sems):
    g = lax.axis_index("grp")
    b = lax.axis_index("blk")
    h = g % 2
    c = b % 2
    x = b // 8
    y = (b // 2) % 4
    pa = x * (1 - c) + y * c
    pb = y * (1 - c) + x * c
    wa = 8 - 6 * c
    wb = 2 + 6 * c

    def blk(da, db):
        return ((pa + da) % 4) * wa + ((pb + db) % 4) * wb + c

    def blk_p(da, db):
        return ((pb + da) % 4) * wb + ((pa + db) % 4) * wa + 1 - c

    def to(bb):
        return {"blk": bb}

    a_up, a_dn, b_up, b_dn, b_far = to(blk(1, 0)), to(blk(3, 0)), to(blk(0, 1)), to(blk(0, 3)), to(blk(0, 2))
    partner = to(b + 1 - 2 * c)
    sibling = {"grp": g + 1 - 2 * h}

    load_tile = pltpu.make_async_copy(tile_hbm.at[0], tile, local_sems.at[0])
    load_low = pltpu.make_async_copy(low_hbm.at[0], packets.at[b, pl.ds(0, ROWS_L)], local_sems.at[1])
    load_dinv = pltpu.make_async_copy(dinv_hbm.at[0], packets.at[b, pl.ds(ROWS_L, ROWS_D)], local_sems.at[2])
    load_idx = pltpu.make_async_copy(idx_hbm, idx, local_sems.at[3])
    load_idx.start()
    load_low.start()
    load_dinv.start()
    load_tile.start()

    barrier = pltpu.get_barrier_semaphore()
    peers = (a_up, a_dn, b_up, b_dn, b_far, partner, sibling)
    for peer in peers:
        pl.semaphore_signal(barrier, inc=1, device_id=peer, device_id_type=MESH)
    pl.semaphore_wait(barrier, len(peers))

    started = []
    names = {}

    def message(name, src, dst, device):
        m = names.setdefault(name, len(names))
        return pltpu.make_async_remote_copy(
            src_ref=src, dst_ref=dst, send_sem=send_sems.at[m], recv_sem=recv_sems.at[m],
            device_id=device, device_id_type=MESH)

    def send(name, src, dst, device):
        copy = message(name, src, dst, device)
        copy.start()
        started.append(copy)

    def receive(name, dst, device):
        message(name, dst, dst, device).wait_recv()

    def slot(k, half=None):
        if half is None:
            return packets.at[k]
        return packets.at[k, pl.ds(half * HALF, HALF)]

    load_idx.wait()
    send("idx", idx, idx_sib, sibling)
    load_low.wait()
    load_dinv.wait()

    def send_b(da):
        k = blk(da, 0)
        send(("b+", da), slot(k), slot(k), b_up)
        send(("b-", da), slot(k), slot(k), b_dn)

    def hand_over(da, db):
        k = blk(da, db)
        send(("p", da, db), slot(k), slot(k), partner)

    def take_over(da, db):
        receive(("p", da, db), slot(blk_p(da, db)), partner)

    send("a+", slot(b), slot(b), a_up)
    send("a-", slot(b), slot(b), a_dn)
    send_b(0)
    hand_over(0, 0)

    load_tile.wait()

    def pick(idx_ref, store):
        names_here = idx_ref[pl.ds(b // 2, 1), :]
        even, odd = names_here[:, :PAD], names_here[:, PAD:]
        rows_here = even * (1 - c) + odd * c
        row_ids = lax.broadcasted_iota(jnp.int32, (192, PAD), 0) + 192 * b
        row_hot = jnp.where(row_ids == rows_here, 1.0, 0.0).astype(BF16)
        for q in range(4):
            hi, lo = split(tile[:, q * 768:(q + 1) * 768])
            picked[:PAD, q * 768:(q + 1) * 768] = dot_t(row_hot, hi).astype(BF16)
            picked[PAD:, q * 768:(q + 1) * 768] = dot_t(row_hot, lo).astype(BF16)

        col_ids = lax.broadcasted_iota(jnp.int32, (384, 2 * PAD), 0)
        for p in range(8):
            cols = idx_ref[pl.ds(8 * h + p, 1), :]
            col_hot = jnp.where(col_ids + 384 * (8 * h + p) == cols, 1.0, 0.0).astype(BF16)
            both = dot(picked[:, p * 384:(p + 1) * 384], col_hot)
            store(p, both[:PAD], both[PAD:])

    def store_send(p, hi, lo):
        panel_send[p] = (hi + lo)[:ROWS_L]
        send(("s", p), panel_send.at[p], panel_recv.at[p], sibling)

    def store_own(p, hi, lo):
        s_hi[8 * h + p] = hi.astype(BF16)
        s_lo[8 * h + p] = lo.astype(BF16)

    receive("idx", idx_sib, sibling)
    pick(idx_sib, store_send)
    pick(idx, store_own)

    acc[...] = jnp.zeros_like(acc)
    receive("a+", slot(blk(3, 0)), a_dn)
    send("a+h", slot(blk(3, 0), 0), slot(blk(3, 0), 0), a_up)
    send_b(3)
    hand_over(3, 0)
    receive("a-", slot(blk(1, 0)), a_up)
    send("a-h", slot(blk(1, 0), 1), slot(blk(1, 0), 1), a_dn)
    send_b(1)
    hand_over(1, 0)

    def forward_b(da):
        receive(("b+", da), slot(blk(da, 3)), b_dn)
        send(("b+h", da), slot(blk(da, 3), 0), slot(blk(da, 3), 0), b_up)
        hand_over(da, 3)
        receive(("b-", da), slot(blk(da, 1)), b_up)
        send(("b-h", da), slot(blk(da, 1), 1), slot(blk(da, 1), 1), b_dn)
        hand_over(da, 1)

    def finish_b(da):
        receive(("b+h", da), slot(blk(da, 2), 0), b_dn)
        receive(("b-h", da), slot(blk(da, 2), 1), b_up)
        hand_over(da, 2)

    forward_b(0)
    receive("a+h", slot(blk(2, 0), 0), a_dn)
    receive("a-h", slot(blk(2, 0), 1), a_up)
    send_b(2)
    hand_over(2, 0)
    forward_b(3)
    forward_b(1)
    finish_b(0)

    def add_chip(dx, dy):
        i = ((pa + dx) % 4) * (wa // 2) + ((pb + dy) % 4) * (wb // 2)
        e_hi, e_lo = split(packets[2 * i, :PAD])
        o_hi, o_lo = split(packets[2 * i + 1, :PAD])
        l_hi = jnp.concatenate([e_hi, o_hi], axis=0)
        l_lo = jnp.concatenate([e_lo, o_lo], axis=0)
        a_hi, a_lo = s_hi[i], s_lo[i]
        acc[...] += dot(a_hi, l_hi) + dot(a_hi, l_lo) + dot(a_lo, l_hi)
        d_full[pl.ds(48 * i, 24)] = packets[2 * i, ROWS_L:]
        d_full[pl.ds(48 * i + 24, 24)] = packets[2 * i + 1, ROWS_L:]

    group_0_1 = [(0, 0), (3, 0), (1, 0), (0, 3), (0, 1)]
    group_2 = [(2, 0), (3, 3), (3, 1), (1, 3), (1, 1), (0, 2)]
    group_3 = [(2, 3), (2, 1), (3, 2), (1, 2)]

    for p in range(8):
        receive(("s", p), panel_recv.at[p], sibling)
        whole = jnp.concatenate([panel_recv[p], jnp.zeros((PAD - ROWS_L, 2 * PAD), F32)], axis=0)
        hi, lo = split(whole)
        s_hi[8 * (1 - h) + p] = hi
        s_lo[8 * (1 - h) + p] = lo
    for d in group_0_1:
        take_over(*d)
    for d in group_0_1:
        add_chip(*d)

    forward_b(2)
    finish_b(3)
    finish_b(1)
    for d in group_2:
        take_over(*d)
    for d in group_2:
        add_chip(*d)
    finish_b(2)
    for d in group_3:
        take_over(*d)
    for d in group_3:
        add_chip(*d)
    take_over(2, 2)
    add_chip(2, 2)

    stacked = jnp.concatenate([acc[...], packets[b, :PAD]], axis=0)
    m_hi, m_lo = split(stacked)
    d_hi, d_lo = split(d_full[...])
    product = dot(m_hi, d_hi) + dot(m_hi, d_lo) + dot(m_lo, d_hi)
    minus = product[:ROWS_L]
    rows_buf[...] = -minus
    store_rows = pltpu.make_async_copy(rows_buf, rows_out.at[0], local_sems.at[0])
    store_rows.start()
    own_d = packets[b, ROWS_L:]
    left_hi, left_lo = split(jnp.concatenate([product[PAD:PAD + ROWS_L], own_d], axis=0))
    right_hi, right_lo = split(jnp.concatenate([minus, own_d], axis=0))
    total = dot_t(left_hi, right_hi) + dot_t(left_hi, right_lo) + dot_t(left_lo, right_hi)
    part[...] = total.reshape(16, 2, ROWS_D, 768)

    send("r1", part.at[:, 1 - c], r1_recv, partner)
    receive("r1", r1_recv, partner)
    for i in range(16):
        ia = (i // 4) * (1 - c) + (i % 4) * c
        ib = (i % 4) * (1 - c) + (i // 4) * c
        r1[ia, ib] = part[i, c] + r1_recv[i]

    low, high = pl.ds(0, 2), pl.ds(2, 2)
    up, dn, far = (pa + 1) % 4, (pa + 3) % 4, (pa + 2) % 4
    send("ra+1", r1.at[far, low], t1.at[0], a_up)
    send("ra-1", r1.at[far, high], t1.at[1], a_dn)
    send("ra+2a", r1.at[up, high], t2.at[0, high], a_up)
    send("ra-2a", r1.at[dn, low], t2.at[1, low], a_dn)
    receive("ra+1", t1.at[0], a_dn)
    r1[up, low] = r1[up, low] + t1[0]
    send("ra+2b", r1.at[up, low], t2.at[0, low], a_up)
    receive("ra-1", t1.at[1], a_up)
    r1[dn, high] = r1[dn, high] + t1[1]
    send("ra-2b", r1.at[dn, high], t2.at[1, high], a_dn)
    receive("ra+2a", t2.at[0, high], a_dn)
    receive("ra-2a", t2.at[1, low], a_up)
    receive("ra+2b", t2.at[0, low], a_dn)
    receive("ra-2b", t2.at[1, high], a_up)
    r2[...] = r1[pa] + t2[0] + t2[1]
    send("rb+", r2.at[(pb + 1) % 4], t3.at[0], b_up)
    send("rb-", r2.at[(pb + 3) % 4], t3.at[1], b_dn)
    send("rb2", r2.at[(pb + 2) % 4], t3.at[2], b_far)
    receive("rb+", t3.at[0], b_dn)
    receive("rb-", t3.at[1], b_up)
    receive("rb2", t3.at[2], b_far)
    diag_out[0] = r2[pb] + t3[0] + t3[1] + t3[2]
    for copy in started:
        copy.wait_send()
    store_rows.wait()


def shards(ancestor_inv, lower_block, diag_inverse, row_index):
    names = row_index.reshape(32, ROWS_L)
    idx = jnp.pad(names, ((0, 0), (0, PAD - ROWS_L)), constant_values=-1).reshape(16, 2 * PAD)
    any_spec = pl.BlockSpec(memory_space=pl.ANY)
    vmem = pltpu.VMEM
    count = 80
    return pl.pallas_call(
        body,
        out_shape=(jax.ShapeDtypeStruct((1, ROWS_L, 768), F32), jax.ShapeDtypeStruct((1, ROWS_D, 768), F32)),
        in_specs=[any_spec] * 4,
        out_specs=(any_spec, pl.BlockSpec(memory_space=pltpu.VMEM)),
        scratch_shapes=[
            vmem((192, 3072), F32),
            vmem((16, 2 * PAD), jnp.int32),
            vmem((16, 2 * PAD), jnp.int32),
            vmem((2 * PAD, 3072), BF16),
            vmem((8, ROWS_L, 2 * PAD), F32),
            vmem((8, ROWS_L, 2 * PAD), F32),
            vmem((16, PAD, 2 * PAD), BF16),
            vmem((16, PAD, 2 * PAD), BF16),
            vmem((32, PACK, 768), F32),
            vmem((PAD, 768), F32),
            vmem((768, 768), F32),
            vmem((16, 2, ROWS_D, 768), F32),
            vmem((16, ROWS_D, 768), F32),
            vmem((4, 4, ROWS_D, 768), F32),
            vmem((2, 2, ROWS_D, 768), F32),
            vmem((2, 4, ROWS_D, 768), F32),
            vmem((4, ROWS_D, 768), F32),
            vmem((3, ROWS_D, 768), F32),
            vmem((ROWS_L, 768), F32),
            pltpu.SemaphoreType.DMA((4,)),
            pltpu.SemaphoreType.DMA((count,)),
            pltpu.SemaphoreType.DMA((count,)),
        ],
        compiler_params=pltpu.CompilerParams(
            collective_id=0, has_side_effects=True, vmem_limit_bytes=58 * 1024 * 1024),
    )(ancestor_inv, lower_block, diag_inverse, idx)


def solution(mesh):
    in_specs = (P("grp", "blk", None), P("grp", "blk", None), P("grp", "blk", None), P("grp", None))
    out_specs = (P("grp", "blk", None), P("grp", "blk", None))
    return jax.shard_map(shards, mesh=mesh, in_specs=in_specs, out_specs=out_specs, check_vma=False)
```

time: 284 us -> 74.1 us (0.26)
  the two profiles are of different devices: /device:TPU:2 before, /device:TPU:10 now
where the time goes in v1:
time: 74.1 us; the launch traced here: 73.8 us
  Pallas kernels  68.4 us (92%)
  local copies, waits for them, and re-layouts  3.97 us (5%)
  other arithmetic  0.76 us (1%)
    pallas_call x1, Pallas kernels, shards(): pl.pallas_call(body, out_shape=(jax.ShapeDtypeStruct((1, ROWS_L, 768), F3...  68.4 us
    unnamed x2, local copies, waits for them, and re-layouts  3.27 us

profile of v1, /device:TPU:10, one launch (start us, length us, event | category | flops | bytes accessed | tf_op | source)
XLA Modules:
  0.0 73.8 jit_solution(8760899967292545925)
XLA Ops:
  0.6 0.8 %reduce = s32[3840]{0:T(1024)S(1)} reduce(s32[1,3840]{1,0:T(1,128)} %param.7, s32[]{:T(128)} %constant.8), dimensions={0}, to_apply=%param.7.reduce_sub_computation | reduce | bytes 30724 | tf_op args[3]
  1.4 0.1 reshape.10
  1.5 0.6 reshape.11.idx_hbm
  2.1 68.4 %shard_map.59 = (f32[1,120,768]{2,1,0:T(8,128)}, f32[1,24,768]{2,1,0:T(8,128)}) custom-call(f32[1,192,3072]{2,1,0:T(8,128)} %tile_hbm.1, f32[1,120,768]{2,1,0:T(8,128)} %low_hbm.1, f32[1,24,768]{2,1,0:T(8,128)} %dinv_hbm.1, s32[16,256]{1,0:T(8,128)} %reshape.11.idx_hbm), custom_call_target="tpu_custom_call" | custom-call | tf_op jit(solution)/shard_map/pallas_call | solution.py:279
  70.5 1.7 %copy.8 = f32[1,120,768]{2,1,0:T(8,128)} copy(f32[1,120,768]{2,1,0:T(8,128)} %get-tuple-element.4) | data formatting | bytes 737280
  72.3 1.5 %copy.9 = f32[1,24,768]{2,1,0:T(8,128)} copy(f32[1,24,768]{2,1,0:T(8,128)} %get-tuple-element.5) | data formatting | bytes 147456
  (1 shorter events, 0.0 us)

commit v2 on v0

v2 whole, which is shorter than its diff:
```python
import jax
import jax.numpy as jnp
from jax import lax
from jax.experimental import pallas as pl
from jax.experimental.pallas import tpu as pltpu
from jax.sharding import PartitionSpec as P

MESH = pl.DeviceIdType.MESH
F32 = jnp.float32
BF16 = jnp.bfloat16
ROWS_L, ROWS_D = 120, 24
PAD = 128
PAIR = 2 * PAD
W = 256


def split(v):
    hi = v.astype(BF16)
    lo = (v - hi.astype(F32)).astype(BF16)
    return hi, lo


def dot(a, b):
    return jnp.dot(a, b, preferred_element_type=F32)


def dot3(a_hi, a_lo, b_hi, b_lo):
    return dot(a_hi, b_hi) + dot(a_hi, b_lo) + dot(a_lo, b_hi)


def dot_t(a, b):
    return lax.dot_general(a, b, (((0,), (0,)), ((), ())), preferred_element_type=F32)


def body(tile_hbm, low_hbm, dinv_hbm, idx_hbm, rows_out, diag_out,
         tile, raw, raw_sib, idx, idx_sib, picked, panel_send, panel_recv, s_hi, s_lo,
         low_a, low_b, acc_a, acc_b, dbuf, d_hi, d_lo, left_hi, left_lo,
         part, r1_recv, r1, t1, t2, r2, t3, rows_buf,
         local_sems, send_sems, recv_sems):
    g = lax.axis_index("grp")
    b = lax.axis_index("blk")
    h = g % 2
    c = b % 2
    chip = b // 2
    x = b // 8
    y = chip % 4
    pa = x * (1 - c) + y * c
    pb = y * (1 - c) + x * c
    wa = 8 - 6 * c
    wb = 2 + 6 * c

    def blk(da, db):
        return ((pa + da) % 4) * wa + ((pb + db) % 4) * wb + c

    def blk_p(da, db):
        return ((pb + da) % 4) * wb + ((pa + db) % 4) * wa + 1 - c

    def chip_at(da, db):
        return blk(da, db) // 2

    def to(bb):
        return {"blk": bb}

    a_up, a_dn, b_up, b_dn, b_far = to(blk(1, 0)), to(blk(3, 0)), to(blk(0, 1)), to(blk(0, 3)), to(blk(0, 2))
    partner = to(b + 1 - 2 * c)
    sibling = {"grp": g + 1 - 2 * h}

    def low_piece(name, ref):
        def slot(k, half):
            first = ROWS_L * (k % 2)
            if half is None:
                return ref.at[k // 2, pl.ds(first, ROWS_L)]
            return ref.at[k // 2, pl.ds(first + 64 * half, 64 - 8 * half)]
        return (name, None, slot)

    def d_piece(j, first_block):
        def slot(k, half):
            if half is None:
                return dbuf.at[pl.ds(ROWS_D * k, ROWS_D), pl.ds(W * j, W)]
            return dbuf.at[pl.ds(ROWS_D * k, ROWS_D), pl.ds(W * j + W // 2 * half, W // 2)]
        return (("d", j), first_block, slot)

    pieces_d = [d_piece(0, None), d_piece(1, W // ROWS_D), d_piece(2, 2 * W // ROWS_D)]
    stream_a = pieces_d + [low_piece("a", low_a)]
    stream_b = [low_piece("b", low_b)]

    own_a = low_a.at[chip, pl.ds(ROWS_L * c, ROWS_L)]
    own_b = low_b.at[chip, pl.ds(ROWS_L * c, ROWS_L)]
    own_d = dbuf.at[pl.ds(ROWS_D * b, ROWS_D)]
    load_idx = pltpu.make_async_copy(idx_hbm, raw, local_sems.at[0])
    load_a = pltpu.make_async_copy(low_hbm.at[0, :, pl.ds(W, 2 * W)], own_a, local_sems.at[1])
    load_b = pltpu.make_async_copy(low_hbm.at[0, :, pl.ds(0, W)], own_b, local_sems.at[4])
    load_tile = pltpu.make_async_copy(tile_hbm.at[0], tile, local_sems.at[2])
    load_d = pltpu.make_async_copy(dinv_hbm.at[0], own_d, local_sems.at[3])
    load_idx.start()
    load_a.start()
    load_tile.start()
    load_b.start()
    dbuf[...] = jnp.zeros_like(dbuf)
    load_d.start()
    low_a[:, 2 * ROWS_L:, :] = jnp.zeros((16, PAIR - 2 * ROWS_L, 2 * W), F32)
    low_b[:, 2 * ROWS_L:, :] = jnp.zeros((16, PAIR - 2 * ROWS_L, W), F32)

    barrier = pltpu.get_barrier_semaphore()
    peers = (a_up, a_dn, b_up, b_dn, b_far, partner, sibling)
    for peer in peers:
        pl.semaphore_signal(barrier, inc=1, device_id=peer, device_id_type=MESH)
    pl.semaphore_wait(barrier, len(peers))

    started = []
    names = {}

    def message(name, src, dst, device):
        m = names.setdefault(name, len(names))
        return pltpu.make_async_remote_copy(
            src_ref=src, dst_ref=dst, send_sem=send_sems.at[m], recv_sem=recv_sems.at[m],
            device_id=device, device_id_type=MESH)

    def when(pred, run):
        if pred is None:
            run()
        else:
            pl.when(pred)(run)

    def send(name, src, dst, device, pred=None):
        copy = message(name, src, dst, device)
        when(pred, copy.start)
        started.append((copy, pred))

    def receive(name, dst, device, pred=None):
        when(pred, message(name, dst, dst, device).wait_recv)

    def send_all(stream, tag, k, half, device):
        for name, first, slot in stream:
            pred = None if first is None else k >= first
            send((name, tag), slot(k, half), slot(k, half), device, pred)

    def receive_all(stream, tag, k, half, device):
        for name, first, slot in stream:
            pred = None if first is None else k >= first
            receive((name, tag), slot(k, half), device, pred)

    def send_b(s, da):
        send_all(s, ("b+", da), blk(da, 0), None, b_up)
        send_all(s, ("b-", da), blk(da, 0), None, b_dn)

    def hand_over(s, da, db):
        send_all(s, ("p", da, db), blk(da, db), None, partner)

    def take_over(s, da, db):
        receive_all(s, ("p", da, db), blk_p(da, db), None, partner)

    def own(s):
        send_all(s, "a+", b, None, a_up)
        send_all(s, "a-", b, None, a_dn)
        send_b(s, 0)
        hand_over(s, 0, 0)

    def forward_b(s, da):
        receive_all(s, ("b+", da), blk(da, 3), None, b_dn)
        send_all(s, ("b+h", da), blk(da, 3), 0, b_up)
        hand_over(s, da, 3)
        receive_all(s, ("b-", da), blk(da, 1), None, b_up)
        send_all(s, ("b-h", da), blk(da, 1), 1, b_dn)
        hand_over(s, da, 1)

    def finish_b(s, da):
        receive_all(s, ("b+h", da), blk(da, 2), 0, b_dn)
        receive_all(s, ("b-h", da), blk(da, 2), 1, b_up)
        hand_over(s, da, 2)

    def group_1(s):
        receive_all(s, "a+", blk(3, 0), None, a_dn)
        send_all(s, "a+h", blk(3, 0), 0, a_up)
        send_b(s, 3)
        hand_over(s, 3, 0)
        receive_all(s, "a-", blk(1, 0), None, a_up)
        send_all(s, "a-h", blk(1, 0), 1, a_dn)
        send_b(s, 1)
        hand_over(s, 1, 0)
        forward_b(s, 0)

    def group_2(s):
        receive_all(s, "a+h", blk(2, 0), 0, a_dn)
        receive_all(s, "a-h", blk(2, 0), 1, a_up)
        send_b(s, 2)
        hand_over(s, 2, 0)
        forward_b(s, 3)
        forward_b(s, 1)
        finish_b(s, 0)

    def group_3(s):
        forward_b(s, 2)
        finish_b(s, 3)
        finish_b(s, 1)

    first_five = [(0, 0), (3, 0), (1, 0), (0, 3), (0, 1)]
    next_six = [(2, 0), (3, 3), (3, 1), (1, 3), (1, 1), (0, 2)]
    last_five = [(2, 3), (2, 1), (3, 2), (1, 2), (2, 2)]

    load_a.wait()
    load_d.wait()
    own(stream_a)
    load_idx.wait()
    send("idx", raw, raw_sib, sibling)

    def widen(raw_ref, idx_ref):
        pad = jnp.full((1, PAIR - 2 * ROWS_L), -1, jnp.int32)
        for i in range(16):
            names_i = raw_ref[:, 2 * ROWS_L * i:2 * ROWS_L * (i + 1)]
            idx_ref[i:i + 1, :] = jnp.concatenate([names_i, pad], axis=1)

    def pick(idx_ref, store):
        names_here = idx_ref[pl.ds(chip, 1), :]
        even, odd = names_here[:, :PAD], names_here[:, ROWS_L:ROWS_L + PAD]
        rows_here = even * (1 - c) + odd * c
        row_ids = lax.broadcasted_iota(jnp.int32, (192, PAD), 0) + 192 * b
        row_hot = jnp.where(row_ids == rows_here, 1.0, 0.0).astype(BF16)
        for q in range(4):
            hi, lo = split(tile[:, q * 768:(q + 1) * 768])
            picked[:PAD, q * 768:(q + 1) * 768] = dot_t(row_hot, hi).astype(BF16)
            picked[PAD:, q * 768:(q + 1) * 768] = dot_t(row_hot, lo).astype(BF16)

        col_ids = lax.broadcasted_iota(jnp.int32, (384, PAIR), 0)
        for p in range(8):
            cols = idx_ref[pl.ds(8 * h + p, 1), :]
            col_hot = jnp.where(col_ids + 384 * (8 * h + p) == cols, 1.0, 0.0).astype(BF16)
            both = dot(picked[:, p * 384:(p + 1) * 384], col_hot)
            store(p, both[:PAD], both[PAD:])

    def store_send(p, hi, lo):
        panel_send[p] = (hi + lo)[:ROWS_L]
        send(("s", p), panel_send.at[p], panel_recv.at[p], sibling)

    def store_own(p, hi, lo):
        s_hi[8 * h + p] = hi.astype(BF16)
        s_lo[8 * h + p] = lo.astype(BF16)

    load_tile.wait()
    receive("idx", raw_sib, sibling)
    widen(raw_sib, idx_sib)
    pick(idx_sib, store_send)
    widen(raw, idx)
    pick(idx, store_own)
    acc_a[...] = jnp.zeros_like(acc_a)
    acc_b[...] = jnp.zeros_like(acc_b)

    group_1(stream_a)
    load_b.wait()
    own(stream_b)
    group_2(stream_a)
    group_1(stream_b)

    def add_chips(stream, low, acc, group):
        for d in group:
            take_over(stream, *d)
        for d in group:
            i = chip_at(*d)
            l_hi, l_lo = split(low[i])
            acc[...] += dot3(s_hi[i], s_lo[i], l_hi, l_lo)

    group_3(stream_a)
    for p in range(8):
        receive(("s", p), panel_recv.at[p], sibling)
        whole = jnp.concatenate([panel_recv[p], jnp.zeros((PAD - ROWS_L, PAIR), F32)], axis=0)
        hi, lo = split(whole)
        s_hi[8 * (1 - h) + p] = hi
        s_lo[8 * (1 - h) + p] = lo
    add_chips(stream_a, low_a, acc_a, first_five)
    group_2(stream_b)
    add_chips(stream_a, low_a, acc_a, next_six)
    finish_b(stream_a, 2)
    add_chips(stream_a, low_a, acc_a, last_five)

    hi, lo = split(dbuf[...])
    d_hi[...] = hi
    d_lo[...] = lo
    fa_hi, fa_lo = split(own_a[...])
    fb_hi, fb_lo = split(own_b[...])
    factor = (dot3(fa_hi, fa_lo, d_hi[W:], d_lo[W:])
              + dot3(fb_hi, fb_lo, d_hi[:W], d_lo[:W]))
    hi, lo = split(jnp.concatenate([factor, own_d[...]], axis=0).T)
    left_hi[...] = hi
    left_lo[...] = lo
    group_3(stream_b)

    near, away = pl.ds(0, 2), pl.ds(2, 2)
    up, dn, far = (pa + 1) % 4, (pa + 3) % 4, (pa + 2) % 4

    def sum_steps(j):
        cols = slice(W * j, W * (j + 1))

        def step_0():
            first = max(W, W * j)
            m_hi, m_lo = split(acc_a[:, first - W:])
            product = dot3(m_hi, m_lo, d_hi[first:, cols], d_lo[first:, cols])
            if j == 0:
                m_hi, m_lo = split(acc_b[...])
                product += dot3(m_hi, m_lo, d_hi[:W, cols], d_lo[:W, cols])
            product = product[:ROWS_L]
            right_hi, right_lo = split(jnp.concatenate([product, own_d[:, cols]], axis=0))
            part[j] = dot3(left_hi[...], left_lo[...], right_hi, right_lo).reshape(16, 2, ROWS_D, W)
            send((j, "r1"), part.at[j, :, 1 - c], r1_recv.at[j], partner)
            rows_buf[:, cols] = -product

        def step_1():
            receive((j, "r1"), r1_recv.at[j], partner)
            for i in range(16):
                ia = (i // 4) * (1 - c) + (i % 4) * c
                ib = (i % 4) * (1 - c) + (i // 4) * c
                r1[j, ia, ib] = part[j, i, c] + r1_recv[j, i]
            send((j, "ra+1"), r1.at[j, far, near], t1.at[j, 0], a_up)
            send((j, "ra-1"), r1.at[j, far, away], t1.at[j, 1], a_dn)
            send((j, "ra+2a"), r1.at[j, up, away], t2.at[j, 0, away], a_up)
            send((j, "ra-2a"), r1.at[j, dn, near], t2.at[j, 1, near], a_dn)

        def step_2():
            receive((j, "ra+1"), t1.at[j, 0], a_dn)
            r1[j, up, near] = r1[j, up, near] + t1[j, 0]
            send((j, "ra+2b"), r1.at[j, up, near], t2.at[j, 0, near], a_up)
            receive((j, "ra-1"), t1.at[j, 1], a_up)
            r1[j, dn, away] = r1[j, dn, away] + t1[j, 1]
            send((j, "ra-2b"), r1.at[j, dn, away], t2.at[j, 1, away], a_dn)

        def step_3():
            receive((j, "ra+2a"), t2.at[j, 0, away], a_dn)
            receive((j, "ra-2a"), t2.at[j, 1, near], a_up)
            receive((j, "ra+2b"), t2.at[j, 0, near], a_dn)
            receive((j, "ra-2b"), t2.at[j, 1, away], a_up)
            r2[j] = r1[j, pa] + t2[j, 0] + t2[j, 1]
            send((j, "rb2"), r2.at[j, (pb + 2) % 4], t3.at[j, 2], b_far)
            send((j, "rb+"), r2.at[j, (pb + 1) % 4], t3.at[j, 0], b_up)
            send((j, "rb-"), r2.at[j, (pb + 3) % 4], t3.at[j, 1], b_dn)

        def step_4():
            receive((j, "rb+"), t3.at[j, 0], b_dn)
            receive((j, "rb-"), t3.at[j, 1], b_up)
            receive((j, "rb2"), t3.at[j, 2], b_far)
            diag_out[0, :, cols] = r2[j, pb] + t3[j, 0] + t3[j, 1] + t3[j, 2]

        return step_0, step_1, step_2, step_3, step_4

    sums = [sum_steps(j) for j in (2, 1, 0)]
    sums[0][0]()
    sums[1][0]()
    add_chips(stream_b, low_b, acc_b, first_five + next_six)
    sums[0][1]()
    sums[1][1]()
    finish_b(stream_b, 2)
    add_chips(stream_b, low_b, acc_b, last_five)
    sums[2][0]()
    store_rows = pltpu.make_async_copy(rows_buf, rows_out.at[0], local_sems.at[0])
    store_rows.start()
    for piece, step in ((0, 2), (1, 2), (2, 1), (0, 3), (1, 3), (2, 2), (0, 4), (2, 3), (1, 4), (2, 4)):
        sums[piece][step]()
    for copy, pred in started:
        when(pred, copy.wait_send)
    store_rows.wait()


def shards(ancestor_inv, lower_block, diag_inverse, row_index):
    any_spec = pl.BlockSpec(memory_space=pl.ANY)
    vmem = pltpu.VMEM
    count = 224
    return pl.pallas_call(
        body,
        out_shape=(jax.ShapeDtypeStruct((1, ROWS_L, 768), F32), jax.ShapeDtypeStruct((1, ROWS_D, 768), F32)),
        in_specs=[any_spec] * 4,
        out_specs=(any_spec, pl.BlockSpec(memory_space=pltpu.VMEM)),
        scratch_shapes=[
            vmem((192, 3072), F32),
            vmem((1, 3840), jnp.int32),
            vmem((1, 3840), jnp.int32),
            vmem((16, PAIR), jnp.int32),
            vmem((16, PAIR), jnp.int32),
            vmem((PAIR, 3072), BF16),
            vmem((8, ROWS_L, PAIR), F32),
            vmem((8, ROWS_L, PAIR), F32),
            vmem((16, PAD, PAIR), BF16),
            vmem((16, PAD, PAIR), BF16),
            vmem((16, PAIR, 2 * W), F32),
            vmem((16, PAIR, W), F32),
            vmem((PAD, 2 * W), F32),
            vmem((PAD, W), F32),
            vmem((768, 768), F32),
            vmem((768, 768), BF16),
            vmem((768, 768), BF16),
            vmem((768, ROWS_L + ROWS_D), BF16),
            vmem((768, ROWS_L + ROWS_D), BF16),
            vmem((3, 16, 2, ROWS_D, W), F32),
            vmem((3, 16, ROWS_D, W), F32),
            vmem((3, 4, 4, ROWS_D, W), F32),
            vmem((3, 2, 2, ROWS_D, W), F32),
            vmem((3, 2, 4, ROWS_D, W), F32),
            vmem((3, 4, ROWS_D, W), F32),
            vmem((3, 3, ROWS_D, W), F32),
            vmem((ROWS_L, 768), F32),
            pltpu.SemaphoreType.DMA((5,)),
            pltpu.SemaphoreType.DMA((count,)),
            pltpu.SemaphoreType.DMA((count,)),
        ],
        compiler_params=pltpu.CompilerParams(
            collective_id=0, has_side_effects=True, vmem_limit_bytes=58 * 1024 * 1024),
    )(ancestor_inv, lower_block, diag_inverse, row_index)


def solution(mesh):
    in_specs = (P("grp", "blk", None), P("grp", "blk", None), P("grp", "blk", None), P("grp", None))
    out_specs = (P("grp", "blk", None), P("grp", "blk", None))
    return jax.shard_map(shards, mesh=mesh, in_specs=in_specs, out_specs=out_specs, check_vma=False)
```

time: 284 us -> 71.6 us (0.25)
  the two profiles are of different devices: /device:TPU:2 before, /device:TPU:32 now
where the time goes in v2:
time: 71.6 us; the launch traced here: 71.3 us
  Pallas kernels  67.4 us (94%)
  local copies, waits for them, and re-layouts  3.27 us (5%)
    pallas_call x1, Pallas kernels, shards(): pl.pallas_call(body, out_shape=(jax.ShapeDtypeStruct((1, ROWS_L, 768), F3...  67.4 us
    unnamed x2, local copies, waits for them, and re-layouts  3.27 us

profile of v2, /device:TPU:32, one launch (start us, length us, event | category | flops | bytes accessed | tf_op | source)
XLA Modules:
  0.0 71.3 jit_solution(10202329090251279577)
XLA Ops:
  0.6 67.4 %shard_map.59 = (f32[1,120,768]{2,1,0:T(8,128)}, f32[1,24,768]{2,1,0:T(8,128)}) custom-call(f32[1,192,3072]{2,1,0:T(8,128)} %tile_hbm.1, f32[1,120,768]{2,1,0:T(8,128)} %low_hbm.1, f32[1,24,768]{2,1,0:T(8,128)} %dinv_hbm.1, s32[1,3840]{1,0:T(1,128)} %idx_hbm.1), custom_call_target="tpu_custom_call" | custom-call | tf_op jit(solution)/shard_map/pallas_call | solution.py:365
  68.1 1.7 %copy.8 = f32[1,120,768]{2,1,0:T(8,128)} copy(f32[1,120,768]{2,1,0:T(8,128)} %get-tuple-element.4) | data formatting | bytes 737280
  69.8 1.5 %copy.9 = f32[1,24,768]{2,1,0:T(8,128)} copy(f32[1,24,768]{2,1,0:T(8,128)} %get-tuple-element.5) | data formatting | bytes 147456

commit v3 on v2

--- a/solution.py
+++ b/solution.py
@@ -28,12 +28,18 @@
     return dot(a_hi, b_hi) + dot(a_hi, b_lo) + dot(a_lo, b_hi)
 
 
+def dot3s(a_both, b_hi, b_lo):
+    n = a_both.shape[0] // 2
+    first = dot(a_both, b_hi)
+    return first[:n] + first[n:] + dot(a_both[:n], b_lo)
+
+
 def dot_t(a, b):
     return lax.dot_general(a, b, (((0,), (0,)), ((), ())), preferred_element_type=F32)
 
 
 def body(tile_hbm, low_hbm, dinv_hbm, idx_hbm, rows_out, diag_out,
-         tile, raw, raw_sib, idx, idx_sib, picked, panel_send, panel_recv, s_hi, s_lo,
+         tile, raw, raw_sib, idx, idx_sib, picked, panel_send, panel_recv, s_both,
          low_a, low_b, acc_a, acc_b, dbuf, d_hi, d_lo, left_hi, left_lo,
          part, r1_recv, r1, t1, t2, r2, t3, rows_buf,
          local_sems, send_sems, recv_sems):
@@ -76,30 +82,32 @@
     def d_piece(j, first_block):
         def slot(k, half):
             if half is None:
-                return dbuf.at[pl.ds(ROWS_D * k, ROWS_D), pl.ds(W * j, W)]
-            return dbuf.at[pl.ds(ROWS_D * k, ROWS_D), pl.ds(W * j + W // 2 * half, W // 2)]
+                return dbuf.at[j, pl.ds(ROWS_D * k, ROWS_D)]
+            return dbuf.at[j, pl.ds(ROWS_D * k + 16 * half, 16 - 8 * half)]
         return (("d", j), first_block, slot)
 
     pieces_d = [d_piece(0, None), d_piece(1, W // ROWS_D), d_piece(2, 2 * W // ROWS_D)]
-    stream_a = pieces_d + [low_piece("a", low_a)]
+    stream_a = [low_piece("a", low_a)] + pieces_d
     stream_b = [low_piece("b", low_b)]
 
     own_a = low_a.at[chip, pl.ds(ROWS_L * c, ROWS_L)]
     own_b = low_b.at[chip, pl.ds(ROWS_L * c, ROWS_L)]
-    own_d = dbuf.at[pl.ds(ROWS_D * b, ROWS_D)]
+    own_rows = pl.ds(ROWS_D * b, ROWS_D)
     load_idx = pltpu.make_async_copy(idx_hbm, raw, local_sems.at[0])
     load_a = pltpu.make_async_copy(low_hbm.at[0, :, pl.ds(W, 2 * W)], own_a, local_sems.at[1])
     load_b = pltpu.make_async_copy(low_hbm.at[0, :, pl.ds(0, W)], own_b, local_sems.at[4])
     load_tile = pltpu.make_async_copy(tile_hbm.at[0], tile, local_sems.at[2])
-    load_d = pltpu.make_async_copy(dinv_hbm.at[0], own_d, local_sems.at[3])
+    loads_d = [
+        pltpu.make_async_copy(dinv_hbm.at[0, :, pl.ds(W * j, W)], dbuf.at[j, own_rows], local_sems.at[5 + j])
+        for j in range(3)]
     load_idx.start()
     load_a.start()
     load_tile.start()
     load_b.start()
-    dbuf[...] = jnp.zeros_like(dbuf)
-    load_d.start()
-    low_a[:, 2 * ROWS_L:, :] = jnp.zeros((16, PAIR - 2 * ROWS_L, 2 * W), F32)
-    low_b[:, 2 * ROWS_L:, :] = jnp.zeros((16, PAIR - 2 * ROWS_L, W), F32)
+    dbuf[1, :W] = jnp.zeros((W, W), F32)
+    dbuf[2, :2 * W] = jnp.zeros((2 * W, W), F32)
+    for load in loads_d:
+        load.start()
 
     barrier = pltpu.get_barrier_semaphore()
     peers = (a_up, a_dn, b_up, b_dn, b_far, partner, sibling)
@@ -108,7 +116,13 @@
     pl.semaphore_wait(barrier, len(peers))
 
     started = []
+    settled = []
     names = {}
+
+    def settle(upto):
+        for copy, pred in started[len(settled):upto]:
+            when(pred, copy.wait_send)
+            settled.append(copy)
 
     def message(name, src, dst, device):
         m = names.setdefault(name, len(names))
@@ -140,66 +154,77 @@
             pred = None if first is None else k >= first
             receive((name, tag), slot(k, half), device, pred)
 
+    def take_over(s, da, db):
+        receive_all(s, ("p", da, db), blk_p(da, db), None, partner)
+
+    def hand_over(s, members):
+        for da, db in members:
+            send_all(s, ("p", da, db), blk(da, db), None, partner)
+
     def send_b(s, da):
         send_all(s, ("b+", da), blk(da, 0), None, b_up)
         send_all(s, ("b-", da), blk(da, 0), None, b_dn)
 
-    def hand_over(s, da, db):
-        send_all(s, ("p", da, db), blk(da, db), None, partner)
-
-    def take_over(s, da, db):
-        receive_all(s, ("p", da, db), blk_p(da, db), None, partner)
-
-    def own(s):
-        send_all(s, "a+", b, None, a_up)
-        send_all(s, "a-", b, None, a_dn)
-        send_b(s, 0)
-        hand_over(s, 0, 0)
-
     def forward_b(s, da):
         receive_all(s, ("b+", da), blk(da, 3), None, b_dn)
         send_all(s, ("b+h", da), blk(da, 3), 0, b_up)
-        hand_over(s, da, 3)
         receive_all(s, ("b-", da), blk(da, 1), None, b_up)
         send_all(s, ("b-h", da), blk(da, 1), 1, b_dn)
-        hand_over(s, da, 1)
 
     def finish_b(s, da):
         receive_all(s, ("b+h", da), blk(da, 2), 0, b_dn)
         receive_all(s, ("b-h", da), blk(da, 2), 1, b_up)
-        hand_over(s, da, 2)
-
-    def group_1(s):
-        receive_all(s, "a+", blk(3, 0), None, a_dn)
-        send_all(s, "a+h", blk(3, 0), 0, a_up)
-        send_b(s, 3)
-        hand_over(s, 3, 0)
-        receive_all(s, "a-", blk(1, 0), None, a_up)
-        send_all(s, "a-h", blk(1, 0), 1, a_dn)
-        send_b(s, 1)
-        hand_over(s, 1, 0)
-        forward_b(s, 0)
-
-    def group_2(s):
-        receive_all(s, "a+h", blk(2, 0), 0, a_dn)
-        receive_all(s, "a-h", blk(2, 0), 1, a_up)
-        send_b(s, 2)
-        hand_over(s, 2, 0)
-        forward_b(s, 3)
-        forward_b(s, 1)
-        finish_b(s, 0)
-
-    def group_3(s):
-        forward_b(s, 2)
-        finish_b(s, 3)
-        finish_b(s, 1)
+
+    def own(stream):
+        for piece in stream:
+            s = [piece]
+            send_all(s, "a+", b, None, a_up)
+            send_all(s, "a-", b, None, a_dn)
+            send_b(s, 0)
+        hand_over(stream, [(0, 0)])
+
+    def group_1(stream):
+        for piece in stream:
+            s = [piece]
+            receive_all(s, "a+", blk(3, 0), None, a_dn)
+            send_all(s, "a+h", blk(3, 0), 0, a_up)
+            send_b(s, 3)
+            receive_all(s, "a-", blk(1, 0), None, a_up)
+            send_all(s, "a-h", blk(1, 0), 1, a_dn)
+            send_b(s, 1)
+            forward_b(s, 0)
+        hand_over(stream, [(3, 0), (1, 0), (0, 3), (0, 1)])
+
+    def group_2(stream):
+        for piece in stream:
+            s = [piece]
+            receive_all(s, "a+h", blk(2, 0), 0, a_dn)
+            receive_all(s, "a-h", blk(2, 0), 1, a_up)
+            send_b(s, 2)
+            forward_b(s, 3)
+            forward_b(s, 1)
+            finish_b(s, 0)
+        hand_over(stream, [(2, 0), (3, 3), (3, 1), (1, 3), (1, 1), (0, 2)])
+
+    def group_3(stream):
+        for piece in stream:
+            s = [piece]
+            forward_b(s, 2)
+            finish_b(s, 3)
+            finish_b(s, 1)
+        hand_over(stream, [(2, 3), (2, 1), (3, 2), (1, 2)])
+
+    def group_4(stream):
+        finish_b(stream, 2)
+        hand_over(stream, [(2, 2)])
 
     first_five = [(0, 0), (3, 0), (1, 0), (0, 3), (0, 1)]
     next_six = [(2, 0), (3, 3), (3, 1), (1, 3), (1, 1), (0, 2)]
     last_five = [(2, 3), (2, 1), (3, 2), (1, 2), (2, 2)]
 
     load_a.wait()
-    load_d.wait()
+    for load in loads_d:
+        load.wait()
     own(stream_a)
     load_idx.wait()
     send("idx", raw, raw_sib, sibling)
@@ -233,8 +258,8 @@
         send(("s", p), panel_send.at[p], panel_recv.at[p], sibling)
 
     def store_own(p, hi, lo):
-        s_hi[8 * h + p] = hi.astype(BF16)
-        s_lo[8 * h + p] = lo.astype(BF16)
+        s_both[8 * h + p, :PAD] = hi.astype(BF16)
+        s_both[8 * h + p, PAD:] = lo.astype(BF16)
 
     load_tile.wait()
     receive("idx", raw_sib, sibling)
@@ -242,14 +267,18 @@
     pick(idx_sib, store_send)
     widen(raw, idx)
     pick(idx, store_own)
+    low_a[:, 2 * ROWS_L:, :] = jnp.zeros((16, PAIR - 2 * ROWS_L, 2 * W), F32)
+    low_b[:, 2 * ROWS_L:, :] = jnp.zeros((16, PAIR - 2 * ROWS_L, W), F32)
     acc_a[...] = jnp.zeros_like(acc_a)
     acc_b[...] = jnp.zeros_like(acc_b)
 
     group_1(stream_a)
     load_b.wait()
     own(stream_b)
+    mark_1 = len(started)
     group_2(stream_a)
     group_1(stream_b)
+    mark_2 = len(started)
 
     def add_chips(stream, low, acc, group):
         for d in group:
@@ -257,32 +286,37 @@
         for d in group:
             i = chip_at(*d)
             l_hi, l_lo = split(low[i])
-            acc[...] += dot3(s_hi[i], s_lo[i], l_hi, l_lo)
+            acc[...] += dot3s(s_both[i], l_hi, l_lo)
 
     group_3(stream_a)
     for p in range(8):
         receive(("s", p), panel_recv.at[p], sibling)
         whole = jnp.concatenate([panel_recv[p], jnp.zeros((PAD - ROWS_L, PAIR), F32)], axis=0)
         hi, lo = split(whole)
-        s_hi[8 * (1 - h) + p] = hi
-        s_lo[8 * (1 - h) + p] = lo
+        s_both[8 * (1 - h) + p, :PAD] = hi
+        s_both[8 * (1 - h) + p, PAD:] = lo
     add_chips(stream_a, low_a, acc_a, first_five)
     group_2(stream_b)
+    settle(mark_1)
     add_chips(stream_a, low_a, acc_a, next_six)
-    finish_b(stream_a, 2)
+    mark_3 = len(started)
+    settle(mark_2)
+    group_4(stream_a)
+    group_3(stream_b)
     add_chips(stream_a, low_a, acc_a, last_five)
 
-    hi, lo = split(dbuf[...])
-    d_hi[...] = hi
-    d_lo[...] = lo
+    for j in range(3):
+        hi, lo = split(dbuf[j])
+        d_hi[:, W * j:W * (j + 1)] = hi
+        d_lo[:, W * j:W * (j + 1)] = lo
+    own_d = jnp.concatenate([dbuf[j, own_rows] for j in range(3)], axis=1)
     fa_hi, fa_lo = split(own_a[...])
     fb_hi, fb_lo = split(own_b[...])
     factor = (dot3(fa_hi, fa_lo, d_hi[W:], d_lo[W:])
               + dot3(fb_hi, fb_lo, d_hi[:W], d_lo[:W]))
-    hi, lo = split(jnp.concatenate([factor, own_d[...]], axis=0).T)
+    hi, lo = split(jnp.concatenate([factor, own_d], axis=0).T)
     left_hi[...] = hi
     left_lo[...] = lo
-    group_3(stream_b)
 
     near, away = pl.ds(0, 2), pl.ds(2, 2)
     up, dn, far = (pa + 1) % 4, (pa + 3) % 4, (pa + 2) % 4
@@ -292,16 +326,16 @@
 
         def step_0():
             first = max(W, W * j)
-            m_hi, m_lo = split(acc_a[:, first - W:])
-            product = dot3(m_hi, m_lo, d_hi[first:, cols], d_lo[first:, cols])
+            m_both = jnp.concatenate(split(acc_a[:, first - W:]), axis=0)
+            product = dot3s(m_both, d_hi[first:, cols], d_lo[first:, cols])
             if j == 0:
-                m_hi, m_lo = split(acc_b[...])
-                product += dot3(m_hi, m_lo, d_hi[:W, cols], d_lo[:W, cols])
+                m_both = jnp.concatenate(split(acc_b[...]), axis=0)
+                product += dot3s(m_both, d_hi[:W, cols], d_lo[:W, cols])
             product = product[:ROWS_L]
             right_hi, right_lo = split(jnp.concatenate([product, own_d[:, cols]], axis=0))
             part[j] = dot3(left_hi[...], left_lo[...], right_hi, right_lo).reshape(16, 2, ROWS_D, W)
             send((j, "r1"), part.at[j, :, 1 - c], r1_recv.at[j], partner)
-            rows_buf[:, cols] = -product
+            rows_buf[:, cols] = product
 
         def step_1():
             receive((j, "r1"), r1_recv.at[j], partner)
@@ -346,23 +380,28 @@
     add_chips(stream_b, low_b, acc_b, first_five + next_six)
     sums[0][1]()
     sums[1][1]()
-    finish_b(stream_b, 2)
+    settle(mark_3)
+    group_4(stream_b)
     add_chips(stream_b, low_b, acc_b, last_five)
     sums[2][0]()
     store_rows = pltpu.make_async_copy(rows_buf, rows_out.at[0], local_sems.at[0])
     store_rows.start()
-    for piece, step in ((0, 2), (1, 2), (2, 1), (0, 3), (1, 3), (2, 2), (0, 4), (2, 3), (1, 4), (2, 4)):
+    for piece, step in ((0, 2), (2, 1), (1, 2), (0, 3), (2, 2), (1, 3), (0, 4), (2, 3), (1, 4), (2, 4)):
         sums[piece][step]()
-    for copy, pred in started:
-        when(pred, copy.wait_send)
+    settle(len(started))
     store_rows.wait()
+
+
+def negate(rows_ref, diag_ref, rows_out, diag_out):
+    rows_out[...] = -rows_ref[...]
+    diag_out[...] = diag_ref[...]
 
 
 def shards(ancestor_inv, lower_block, diag_inverse, row_index):
     any_spec = pl.BlockSpec(memory_space=pl.ANY)
     vmem = pltpu.VMEM
     count = 224
-    return pl.pallas_call(
+    rows, diag = pl.pallas_call(
         body,
         out_shape=(jax.ShapeDtypeStruct((1, ROWS_L, 768), F32), jax.ShapeDtypeStruct((1, ROWS_D, 768), F32)),
         in_specs=[any_spec] * 4,
@@ -376,13 +415,12 @@
             vmem((PAIR, 3072), BF16),
             vmem((8, ROWS_L, PAIR), F32),
             vmem((8, ROWS_L, PAIR), F32),
-            vmem((16, PAD, PAIR), BF16),
-            vmem((16, PAD, PAIR), BF16),
+            vmem((16, 2 * PAD, PAIR), BF16),
             vmem((16, PAIR, 2 * W), F32),
             vmem((16, PAIR, W), F32),
             vmem((PAD, 2 * W), F32),
             vmem((PAD, W), F32),
-            vmem((768, 768), F32),
+            vmem((3, 768, W), F32),
             vmem((768, 768), BF16),
             vmem((768, 768), BF16),
             vmem((768, ROWS_L + ROWS_D), BF16),
@@ -395,13 +433,17 @@
             vmem((3, 4, ROWS_D, W), F32),
             vmem((3, 3, ROWS_D, W), F32),
             vmem((ROWS_L, 768), F32),
-            pltpu.SemaphoreType.DMA((5,)),
+            pltpu.SemaphoreType.DMA((8,)),
             pltpu.SemaphoreType.DMA((count,)),
             pltpu.SemaphoreType.DMA((count,)),
         ],
         compiler_params=pltpu.CompilerParams(
             collective_id=0, has_side_effects=True, vmem_limit_bytes=58 * 1024 * 1024),
     )(ancestor_inv, lower_block, diag_inverse, row_index)
+    return pl.pallas_call(
+        negate,
+        out_shape=(jax.ShapeDtypeStruct(rows.shape, F32), jax.ShapeDtypeStruct(diag.shape, F32)),
+    )(rows, diag)
 
 
 def solution(mesh):

time: 71.6 us -> 69.4 us (0.969)
  the two profiles are of different devices: /device:TPU:32 before, /device:TPU:192 now
where the time goes in v3:
time: 69.4 us; the launch traced here: 69.2 us
  Pallas kernels  68.6 us (99%)
    pallas_call x1, Pallas kernels, shards(): pl.pallas_call(body, out_shape=(jax.ShapeDtypeStruct((1, ROWS_L, 768), F3...  66.8 us
    pallas_call x1, Pallas kernels, shards(): pl.pallas_call(negate, out_shape=(jax.ShapeDtypeStruct(rows.shape, F32),...  1.78 us

profile of v3, /device:TPU:192, one launch (start us, length us, event | category | flops | bytes accessed | tf_op | source)
XLA Modules:
  0.0 69.2 jit_solution(15181237184260936106)
XLA Ops:
  0.6 66.8 %shard_map.59 = (f32[1,120,768]{2,1,0:T(8,128)}, f32[1,24,768]{2,1,0:T(8,128)}) custom-call(f32[1,192,3072]{2,1,0:T(8,128)} %tile_hbm.1, f32[1,120,768]{2,1,0:T(8,128)} %low_hbm.1, f32[1,24,768]{2,1,0:T(8,128)} %dinv_hbm.1, s32[1,3840]{1,0:T(1,128)} %idx_hbm.1), custom_call_target="tpu_custom_call" | custom-call | tf_op jit(solution)/shard_map/pallas_call | solution.py:404
  67.4 1.8 %shard_map.60 = (f32[1,120,768]{2,1,0:T(8,128)}, f32[1,24,768]{2,1,0:T(8,128)}) custom-call(f32[1,120,768]{2,1,0:T(8,128)} %get-tuple-element.4.rows_ref, f32[1,24,768]{2,1,0:T(8,128)} %get-tuple-element.5.diag_ref), custom_call_target="tpu_custom_call" | custom-call | tf_op jit(solution)/shard_map/pallas_call | solution.py:443

commit v4 on v3

--- a/solution.py
+++ b/solution.py
@@ -79,33 +79,39 @@
             return ref.at[k // 2, pl.ds(first + 64 * half, 64 - 8 * half)]
         return (name, None, slot)
 
-    def d_piece(j, first_block):
+    def d_piece(pieces):
+        size = ROWS_D * pieces
+        split_at = size // 16 * 8
+
         def slot(k, half):
             if half is None:
-                return dbuf.at[j, pl.ds(ROWS_D * k, ROWS_D)]
-            return dbuf.at[j, pl.ds(ROWS_D * k + 16 * half, 16 - 8 * half)]
-        return (("d", j), first_block, slot)
-
-    pieces_d = [d_piece(0, None), d_piece(1, W // ROWS_D), d_piece(2, 2 * W // ROWS_D)]
+                return dbuf.at[k, pl.ds(0, size)]
+            return dbuf.at[k, pl.ds(half * split_at, split_at + half * (size - 2 * split_at))]
+
+        def has(k):
+            enough = k >= (0, W // ROWS_D, 2 * W // ROWS_D)[pieces - 1]
+            return enough if pieces == 3 else jnp.logical_and(enough, k < (W // ROWS_D, 2 * W // ROWS_D)[pieces - 1])
+        return ("d", has, slot)
+
+    pieces_d = [d_piece(1), d_piece(2), d_piece(3)]
     stream_a = [low_piece("a", low_a)] + pieces_d
     stream_b = [low_piece("b", low_b)]
 
     own_a = low_a.at[chip, pl.ds(ROWS_L * c, ROWS_L)]
     own_b = low_b.at[chip, pl.ds(ROWS_L * c, ROWS_L)]
-    own_rows = pl.ds(ROWS_D * b, ROWS_D)
     load_idx = pltpu.make_async_copy(idx_hbm, raw, local_sems.at[0])
     load_a = pltpu.make_async_copy(low_hbm.at[0, :, pl.ds(W, 2 * W)], own_a, local_sems.at[1])
     load_b = pltpu.make_async_copy(low_hbm.at[0, :, pl.ds(0, W)], own_b, local_sems.at[4])
     load_tile = pltpu.make_async_copy(tile_hbm.at[0], tile, local_sems.at[2])
     loads_d = [
-        pltpu.make_async_copy(dinv_hbm.at[0, :, pl.ds(W * j, W)], dbuf.at[j, own_rows], local_sems.at[5 + j])
+        pltpu.make_async_copy(dinv_hbm.at[0, :, pl.ds(W * j, W)], dbuf.at[b, pl.ds(ROWS_D * j, ROWS_D)], local_sems.at[5 + j])
         for j in range(3)]
     load_idx.start()
     load_a.start()
     load_tile.start()
     load_b.start()
-    dbuf[1, :W] = jnp.zeros((W, W), F32)
-    dbuf[2, :2 * W] = jnp.zeros((2 * W, W), F32)
+    dbuf[:W // ROWS_D, ROWS_D:] = jnp.zeros((W // ROWS_D, 2 * ROWS_D, W), F32)
+    dbuf[W // ROWS_D:2 * W // ROWS_D, 2 * ROWS_D:] = jnp.zeros((2 * W // ROWS_D - W // ROWS_D, ROWS_D, W), F32)
     for load in loads_d:
         load.start()
 
@@ -146,12 +152,12 @@
 
     def send_all(stream, tag, k, half, device):
         for name, first, slot in stream:
-            pred = None if first is None else k >= first
+            pred = None if first is None else first(k)
             send((name, tag), slot(k, half), slot(k, half), device, pred)
 
     def receive_all(stream, tag, k, half, device):
         for name, first, slot in stream:
-            pred = None if first is None else k >= first
+            pred = None if first is None else first(k)
             receive((name, tag), slot(k, half), device, pred)
 
     def take_over(s, da, db):
@@ -306,10 +312,10 @@
     add_chips(stream_a, low_a, acc_a, last_five)
 
     for j in range(3):
-        hi, lo = split(dbuf[j])
+        hi, lo = split(dbuf[:, ROWS_D * j:ROWS_D * (j + 1)].reshape(768, W))
         d_hi[:, W * j:W * (j + 1)] = hi
         d_lo[:, W * j:W * (j + 1)] = lo
-    own_d = jnp.concatenate([dbuf[j, own_rows] for j in range(3)], axis=1)
+    own_d = jnp.concatenate([dbuf[b, pl.ds(ROWS_D * j, ROWS_D)] for j in range(3)], axis=1)
     fa_hi, fa_lo = split(own_a[...])
     fb_hi, fb_lo = split(own_b[...])
     factor = (dot3(fa_hi, fa_lo, d_hi[W:], d_lo[W:])
@@ -420,7 +426,7 @@
             vmem((16, PAIR, W), F32),
             vmem((PAD, 2 * W), F32),
             vmem((PAD, W), F32),
-            vmem((3, 768, W), F32),
+            vmem((32, 3 * ROWS_D, W), F32),
             vmem((768, 768), BF16),
             vmem((768, 768), BF16),
             vmem((768, ROWS_L + ROWS_D), BF16),

time: 69.4 us -> 68.7 us (0.990)
  Pallas kernels: 68.6 us -> 67.9 us
where the time goes in v4:
time: 68.7 us; the launch traced here: 68.5 us
  Pallas kernels  67.9 us (99%)
    pallas_call x1, Pallas kernels, shards(): pl.pallas_call(body, out_shape=(jax.ShapeDtypeStruct((1, ROWS_L, 768), F3...  66.1 us
    pallas_call x1, Pallas kernels, shards(): pl.pallas_call(negate, out_shape=(jax.ShapeDtypeStruct(rows.shape, F32),...  1.78 us

profile of v4, /device:TPU:192, one launch (start us, length us, event | category | flops | bytes accessed | tf_op | source)
XLA Modules:
  0.0 68.5 jit_solution(2422558433525677642)
XLA Ops:
  0.6 66.1 %shard_map.59 = (f32[1,120,768]{2,1,0:T(8,128)}, f32[1,24,768]{2,1,0:T(8,128)}) custom-call(f32[1,192,3072]{2,1,0:T(8,128)} %tile_hbm.1, f32[1,120,768]{2,1,0:T(8,128)} %low_hbm.1, f32[1,24,768]{2,1,0:T(8,128)} %dinv_hbm.1, s32[1,3840]{1,0:T(1,128)} %idx_hbm.1), custom_call_target="tpu_custom_call" | custom-call | tf_op jit(solution)/shard_map/pallas_call | solution.py:410
  66.7 1.8 %shard_map.60 = (f32[1,120,768]{2,1,0:T(8,128)}, f32[1,24,768]{2,1,0:T(8,128)}) custom-call(f32[1,120,768]{2,1,0:T(8,128)} %get-tuple-element.4.rows_ref, f32[1,24,768]{2,1,0:T(8,128)} %get-tuple-element.5.diag_ref), custom_call_target="tpu_custom_call" | custom-call | tf_op jit(solution)/shard_map/pallas_call | solution.py:449
